TPU v7x, 32 devices: a whole 2x2x4 slice. The times are simulated.
32 devices in a mesh: space: 2 (over core), energy: 8 (over z, y), mom: 2 (over x).
Axes of the slice: x: 2, y: 2, z: 4, core: 2. Of those that a mesh axis runs over, the one named last changes fastest.
Arguments:
- hamiltonian: float32 [2, 256, 256], P('space'), may hold values from -0.375 to 0.375
- coupling: float32 [2, 224, 224], P('space'), may hold values from -0.75 to 0.75
- self_energy: float32 [2, 8, 4, 2, 256, 256], P('space', 'energy', 'mom'), may hold values from -0.375 to 0.375
- pattern: int32 [2, 256, 256], P('space', 'energy'), may hold values 0 or 1
- momentum_table: int32 [4, 4], replicated, may hold values from 0 to 3
- momentum_weights: float32 [4], replicated, may hold values from 0.2 to 1
- mode_strengths: float32 [2], replicated, may hold values from 0.3 to 1
- mode_offsets: int32 [2], replicated, may hold values from 1 to 5
Outputs:
- new_self_energy: float32 [2, 8, 4, 2, 256, 256], P('space', 'energy', 'mom')
Inputs may be any that keep to these rules, and one draw needn't show every extreme that they name: `momentum_table`: entry [k, q] is the momentum index whose Green's function reaches momentum k through transfer q.
All inputs are finite; a program needn't handle non-finite values. No bound on the sum of `pattern` on one device may be relied on, other than what follows from the above.
Results may differ from a plain program's by a relative error of at most 0.0001.
Values sent between devices are 32-bit elements; how exact they have to be, the bound alone decides.
No kernel may reach another device: no remote copies, remote signals or barrier semaphores. Data moves between devices by JAX's collectives and lax.ppermute only.
A program may use at most 128 MiB of HBM per device.

v0:
```python
import jax
import jax.numpy as jnp
from jax import lax
from jax.sharding import PartitionSpec as P

broadening = 1.0
contact = 1.0
dispersion = 1.0


def from_behind(shard, axis, by):
    count = lax.axis_size(axis)
    pairs = [(i, i + by) for i in range(count) if 0 <= i + by < count]
    return lax.ppermute(shard, axis, pairs)


def matmul_highest(left_side, right_side):
    return jnp.einsum("...ij,...jk->...ik", left_side, right_side, precision=lax.Precision.HIGHEST)


def product_complex(left_side, right_side):
    left_real = left_side[..., 0, :, :]
    left_imag = left_side[..., 1, :, :]
    right_real = right_side[..., 0, :, :]
    right_imag = right_side[..., 1, :, :]
    real_part = matmul_highest(left_real, right_real) - matmul_highest(left_imag, right_imag)
    imag_part = matmul_highest(left_real, right_imag) + matmul_highest(left_imag, right_real)
    return jnp.stack([real_part, imag_part], axis=-3)


def approximate_inverse(matrix):
    order_size = matrix.shape[-1]
    identity = jnp.eye(order_size, dtype=jnp.float32)
    real_part = matrix[..., 0, :, :]
    imag_part = matrix[..., 1, :, :]
    diag_real = jnp.diagonal(real_part, axis1=-2, axis2=-1)
    diag_imag = jnp.diagonal(imag_part, axis1=-2, axis2=-1)
    modulus = diag_real * diag_real + diag_imag * diag_imag
    inverse_real = diag_real / modulus
    inverse_imag = -diag_imag / modulus
    outside = 1.0 - identity
    off_real = real_part * outside
    off_imag = imag_part * outside
    row_real = inverse_real[..., :, None]
    row_imag = inverse_imag[..., :, None]
    scaled = jnp.stack(
        [row_real * off_real - row_imag * off_imag, row_real * off_imag + row_imag * off_real],
        axis=-3,
    )
    series = product_complex(scaled, scaled) - scaled
    series_real = series[..., 0, :, :] + identity
    series_imag = series[..., 1, :, :]
    column_real = inverse_real[..., None, :]
    column_imag = inverse_imag[..., None, :]
    return jnp.stack(
        [
            series_real * column_real - series_imag * column_imag,
            series_real * column_imag + series_imag * column_real,
        ],
        axis=-3,
    )


def build_system(
    hamiltonian_slice, self_slice, energy_index, momentum_index, energies_all, momenta_all
):
    order_size = hamiltonian_slice.shape[-1]
    identity = jnp.eye(order_size, dtype=jnp.float32)
    symmetric = 0.5 * (hamiltonian_slice + hamiltonian_slice.T)
    energy = -2.0 + 4.0 * energy_index.astype(jnp.float32) / energies_all
    kinetic = dispersion * (
        1.0 - jnp.cos(2.0 * jnp.pi * momentum_index.astype(jnp.float32) / momenta_all)
    )
    diagonal_shift = energy[:, None] - kinetic[None, :]
    real_part = diagonal_shift[:, :, None, None] * identity - symmetric - self_slice[:, :, 0]
    imag_part = broadening * identity - self_slice[:, :, 1]
    return jnp.stack([real_part, imag_part], axis=2)


def contact_term(surface):
    return jnp.stack(
        [jnp.zeros((surface, surface), jnp.float32), -contact * jnp.eye(surface, dtype=jnp.float32)]
    )


def embed_first(matrix, term):
    width = term.shape[-1]
    return matrix.at[..., :width, :width].add(-term)


def embed_last(matrix, term):
    width = term.shape[-1]
    order_size = matrix.shape[-1]
    return matrix.at[..., order_size - width :, order_size - width :].add(-term)


def sandwich(coupling_block, middle):
    return jnp.einsum(
        "ji,...jk,kl->...il",
        coupling_block,
        middle,
        coupling_block,
        precision=lax.Precision.HIGHEST,
    )


def sandwich_back(coupling_block, middle):
    return jnp.einsum(
        "ij,...jk,lk->...il",
        coupling_block,
        middle,
        coupling_block,
        precision=lax.Precision.HIGHEST,
    )


def convolve_energy(green_rows, mode_strengths, mode_offsets):
    point_count = green_rows.shape[0]
    widths = [(point_count, point_count)] + [(0, 0)] * (green_rows.ndim - 1)
    padded = jnp.pad(green_rows, widths)
    accumulated = jnp.zeros_like(green_rows)
    for mode_index in range(mode_strengths.shape[0]):
        offset_now = mode_offsets[mode_index]
        below_part = lax.dynamic_slice_in_dim(padded, point_count - offset_now, point_count, 0)
        above_part = lax.dynamic_slice_in_dim(padded, point_count + offset_now, point_count, 0)
        accumulated = accumulated + mode_strengths[mode_index] * (below_part + above_part)
    return accumulated


def momentum_coefficients(momentum_table, momentum_weights):
    momentum_count = momentum_table.shape[0]
    labels = jnp.arange(momentum_count, dtype=jnp.int32)
    matches = (momentum_table[:, :, None] == labels[None, None, :]).astype(jnp.float32)
    return jnp.einsum("q,kqj->kj", momentum_weights, matches, precision=lax.Precision.HIGHEST)


def keep_state(held_terms, message):
    return (held_terms, message)


def body(
    hamiltonian,
    coupling,
    self_energy,
    pattern,
    momentum_table,
    momentum_weights,
    mode_strengths,
    mode_offsets,
):
    orbitals = hamiltonian.shape[-1]
    surface = coupling.shape[-1]
    energies_here = self_energy.shape[1]
    momenta_here = self_energy.shape[2]
    energy_groups = lax.axis_size("energy")
    momentum_groups = lax.axis_size("mom")
    slices = lax.axis_size("space")
    position = lax.axis_index("space")
    energies_all = energies_here * energy_groups
    momenta_all = momenta_here * momentum_groups
    energy_index = lax.axis_index("energy") * energies_here + jnp.arange(
        energies_here, dtype=jnp.int32
    )
    momentum_index = lax.axis_index("mom") * momenta_here + jnp.arange(
        momenta_here, dtype=jnp.int32
    )
    item_count = energies_here * momenta_here
    system = build_system(
        hamiltonian[0], self_energy[0], energy_index, momentum_index, energies_all, momenta_all
    )
    system = system.reshape(item_count, 2, orbitals, orbitals)
    coupling_block = coupling[0]
    corner = orbitals - surface
    first_slice = position == 0
    last_slice = position == slices - 1
    zero_terms = jnp.zeros((item_count, 2, surface, surface), jnp.float32)
    single_source = contact_term(surface)
    zero_message = jnp.zeros((2, surface, surface), jnp.float32)

    def forward_turn(sweep_step, carry):
        received = from_behind(carry[1], "space", 1)
        item_now = sweep_step - position

        def forward_active(held_terms, message):
            incoming = jnp.where(first_slice, single_source, received)
            current = lax.dynamic_index_in_dim(system, item_now, 0, keepdims=False)
            green_left = approximate_inverse(embed_first(current, incoming))
            stored = lax.dynamic_update_index_in_dim(held_terms, incoming, item_now, 0)
            return (stored, sandwich(coupling_block, green_left[..., corner:, corner:]))

        return lax.cond(
            (item_now >= 0) & (item_now < item_count),
            forward_active,
            keep_state,
            carry[0],
            carry[1],
        )

    def backward_turn(sweep_step, carry):
        received = from_behind(carry[1], "space", -1)
        item_now = sweep_step - (slices - 1 - position)

        def backward_active(held_terms, message):
            incoming = jnp.where(last_slice, single_source, received)
            right_now = sandwich_back(coupling_block, incoming)
            current = lax.dynamic_index_in_dim(system, item_now, 0, keepdims=False)
            green_right = approximate_inverse(embed_last(current, right_now))
            stored = lax.dynamic_update_index_in_dim(held_terms, right_now, item_now, 0)
            return (stored, green_right[..., :surface, :surface])

        return lax.cond(
            (item_now >= 0) & (item_now < item_count),
            backward_active,
            keep_state,
            carry[0],
            carry[1],
        )

    turn_total = slices + item_count - 1
    left_terms, unused_left = lax.fori_loop(0, turn_total, forward_turn, (zero_terms, zero_message))
    right_terms, unused_right = lax.fori_loop(
        0, turn_total, backward_turn, (zero_terms, zero_message)
    )
    green_final = approximate_inverse(embed_last(embed_first(system, left_terms), right_terms))
    coefficients = momentum_coefficients(momentum_table, momentum_weights)
    mask_rows = pattern[0].astype(jnp.float32)
    row_count = orbitals // energy_groups
    blocks = green_final.reshape(energies_here, momenta_here, 2, energy_groups, row_count, orbitals)
    regrouped = lax.all_to_all(blocks, "energy", split_axis=3, concat_axis=0, tiled=True)
    regrouped = regrouped.reshape(energies_all, momenta_here, 2, row_count, orbitals)
    phonon = convolve_energy(regrouped, mode_strengths, mode_offsets)
    own_rows = lax.dynamic_slice_in_dim(
        coefficients, lax.axis_index("mom") * momenta_here, momenta_here, 0
    )
    mixed_terms = jnp.zeros_like(phonon) + jnp.einsum(
        "kj,ej...->ek...",
        own_rows,
        lax.all_gather(phonon, "mom", axis=1, tiled=True),
        precision=lax.Precision.HIGHEST,
    )
    mixed_terms = mixed_terms * mask_rows
    mixed_terms = mixed_terms.reshape(energies_all, momenta_here, 2, 1, row_count, orbitals)
    returned = lax.all_to_all(mixed_terms, "energy", split_axis=0, concat_axis=3, tiled=True)
    return returned.reshape(1, energies_here, momenta_here, 2, orbitals, orbitals)


def solution(mesh):
    return jax.shard_map(
        body,
        mesh=mesh,
        in_specs=(
            P("space", None, None),
            P("space", None, None),
            P("space", "energy", "mom", None, None, None),
            P("space", "energy", None),
            P(),
            P(),
            P(),
            P(),
        ),
        out_specs=P("space", "energy", "mom", None, None, None),
        check_vma=False,
    )
```

profile of v0, /device:TPU:0, one launch (start us, length us, event | category | flops | bytes accessed | tf_op | source)
XLA Modules:
  0.0 275.0 jit_solution(17039815926781231370)
XLA Ops:
  15.1 32.7 %while.36 = (s32[]{:T(128)}, f32[2,2,224,224]{3,2,1,0:T(8,128)}, f32[2,224,224]{2,1,0:T(8,128)S(1)}, s32[]{:T(128)}, pred[]{:T(512)}, /*index=5*/f32[2,224,224]{...) while((s32[]{:T(128)}, f32[2,2,224,224]{3,2,1,0:T(8,128)}, ...), condition=%wide.region_3.0_spmd, body=%wide.region_0.3_spmd.sunk | while | flops 1347138048 | bytes 16336718 | solution.py:220
  15.1 2.4 collective-permute-start
  19.0 11.2 %conditional.4 = ((f32[2,2,224,224]{3,2,1,0:T(8,128)}, f32[2,224,224]{2,1,0:T(8,128)S(1)})) conditional(s32[]{:T(128)} %convert_element_type.173, (f32[2,2,224,224]{3,2,1,0:T(8,128)}, f32[2,224,224]{2,1,0:T(8,128)S(1)}) %tuple.116, (pred[]{:T(512)}, f32[2,224,224]{2,1,0:T(8,128)S(1)}, f32[2,224,224]{2,1,0:T(8,128)S(1)}, s32[]{:T(128)}, ...), branch_computations={%region_1.0_spmd, %region_2.2_spmd} | conditional | flops 1347138048 | bytes 14730827 | solution.py:191
  21.5 2.3 gather_fusion
  23.8 2.3 gather_fusion.1
  32.9 11.3 %conditional.4 = ((f32[2,2,224,224]{3,2,1,0:T(8,128)}, f32[2,224,224]{2,1,0:T(8,128)S(1)})) conditional(s32[]{:T(128)} %convert_element_type.173, (f32[2,2,224,224]{3,2,1,0:T(8,128)}, f32[2,224,224]{2,1,0:T(8,128)S(1)}) %tuple.116, (pred[]{:T(512)}, f32[2,224,224]{2,1,0:T(8,128)S(1)}, f32[2,224,224]{2,1,0:T(8,128)S(1)}, s32[]{:T(128)}, ...), branch_computations={%region_1.0_spmd, %region_2.2_spmd} | conditional | flops 1347138048 | bytes 14730827 | solution.py:191
  35.4 2.3 gather_fusion
  37.8 2.3 gather_fusion.1
  49.4 5.2 %scatter-add.16 = f32[2,2,256,256]{3,2,0,1:T(8,128)} dynamic-update-slice(f32[2,2,256,256]{3,2,0,1:T(8,128)} %copy-done.2, f32[2,2,224,224]{3,2,0,1:T(8,128)S(1)} %fusion.55, s32[]{:T(128)} %constant.266.clone.1, s32[]{:T(128)} %constant.266.clone.1, s32[]{:T(128)} %constant.266.clone.1, s32[]{:T(128)} %constant.266.clone.1) | dynamic-update-slice | bytes 1605636 | tf_op jit(solution)/shard_map/scatter-add | solution.py:88
  55.7 61.7 %while.37 = (s32[]{:T(128)}, f32[2,2,224,224]{3,2,1,0:T(8,128)}, f32[2,224,224]{2,1,0:T(8,128)S(1)}, s32[]{:T(128)}, pred[]{:T(512)}, /*index=5*/f32[2,224,224]{...) while((s32[]{:T(128)}, f32[2,2,224,224]{3,2,1,0:T(8,128)}, ...), condition=%wide.region_7.8_spmd, body=%wide.region_4.7_spmd.sunk | while | flops 1347037696 | bytes 17139036 | solution.py:221
  57.4 13.1 %collective-permute-done.1 = f32[2,224,224]{1,2,0:T(8,128)} collective-permute-done((f32[2,224,224]{1,2,0:T(8,128)S(1)}, f32[2,224,224]{1,2,0:T(8,128)}, u32[]{:S(2)}, u32[]{:S(2)}) %collective-permute-start.1) | collective-permute-done | bytes 401440 | tf_op jit(solution)/shard_map/while/body/eval_jaxpr/ppermute | solution.py:14
  72.0 14.8 %collective-permute-done.1 = f32[2,224,224]{1,2,0:T(8,128)} collective-permute-done((f32[2,224,224]{1,2,0:T(8,128)S(1)}, f32[2,224,224]{1,2,0:T(8,128)}, u32[]{:S(2)}, u32[]{:S(2)}) %collective-permute-start.1) | collective-permute-done | bytes 401440 | tf_op jit(solution)/shard_map/while/body/eval_jaxpr/ppermute | solution.py:14
  86.8 13.3 %conditional.5 = ((f32[2,2,224,224]{3,2,1,0:T(8,128)}, f32[2,224,224]{2,1,0:T(8,128)S(1)})) conditional(s32[]{:T(128)} %convert_element_type.174, (f32[2,2,224,224]{3,2,1,0:T(8,128)}, f32[2,224,224]{2,1,0:T(8,128)S(1)}) %tuple.119, (pred[]{:T(512)}, f32[2,224,224]{1,2,0:T(8,128)}, f32[2,224,224]{1,2,0:T(8,128)}, f32[224,224]{1,0:T(8,128)S(1)}, ...), branch_computations={%region_5.5_spmd, %region_6.6_spmd} | conditional | flops 1347037696 | bytes 14730331 | solution.py:211
  90.0 3.4 %scatter-add.10 = f32[2,256,256]{2,1,0:T(8,128)S(1)} dynamic-update-slice(f32[2,256,256]{2,1,0:T(8,128)S(1)} %dynamic-slice_bitcast_fusion.2, f32[2,224,224]{2,1,0:T(8,128)S(1)} %fusion.22, s32[]{:T(128)} %constant.251.clone, s32[]{:T(128)} %constant.253.clone, s32[]{:T(128)} %constant.253.clone) | dynamic-update-slice | bytes 802820 | tf_op jit(solution)/shard_map/while/body/eval_jaxpr/cond/branch_1_fun/scatter-add | solution.py:94
  93.4 2.3 gather_fusion.2
  95.8 2.3 gather_fusion.3
  101.6 2.5 collective-permute-done.1
  104.1 13.3 %conditional.5 = ((f32[2,2,224,224]{3,2,1,0:T(8,128)}, f32[2,224,224]{2,1,0:T(8,128)S(1)})) conditional(s32[]{:T(128)} %convert_element_type.174, (f32[2,2,224,224]{3,2,1,0:T(8,128)}, f32[2,224,224]{2,1,0:T(8,128)S(1)}) %tuple.119, (pred[]{:T(512)}, f32[2,224,224]{1,2,0:T(8,128)}, f32[2,224,224]{1,2,0:T(8,128)}, f32[224,224]{1,0:T(8,128)S(1)}, ...), branch_computations={%region_5.5_spmd, %region_6.6_spmd} | conditional | flops 1347037696 | bytes 14730331 | solution.py:211
  107.3 3.4 %scatter-add.10 = f32[2,256,256]{2,1,0:T(8,128)S(1)} dynamic-update-slice(f32[2,256,256]{2,1,0:T(8,128)S(1)} %dynamic-slice_bitcast_fusion.2, f32[2,224,224]{2,1,0:T(8,128)S(1)} %fusion.22, s32[]{:T(128)} %constant.251.clone, s32[]{:T(128)} %constant.253.clone, s32[]{:T(128)} %constant.253.clone) | dynamic-update-slice | bytes 802820 | tf_op jit(solution)/shard_map/while/body/eval_jaxpr/cond/branch_1_fun/scatter-add | solution.py:94
  110.8 2.3 gather_fusion.2
  113.2 2.3 gather_fusion.3
  118.9 7.0 %scatter-add.17 = f32[2,2,256,256]{3,2,0,1:T(8,128)S(1)} dynamic-update-slice(f32[2,2,256,256]{3,2,0,1:T(8,128)S(1)} %copy-done.3, f32[2,2,224,224]{3,2,0,1:T(8,128)S(1)} %slice_add_fusion, s32[]{:T(128)} %constant.266.clone.1, s32[]{:T(128)} %constant.266.clone.1, s32[]{:T(128)} %constant.271.clone.1, s32[]{:T(128)} %constant.271.clone.1) | dynamic-update-slice | bytes 1605636 | tf_op jit(solution)/shard_map/scatter-add | solution.py:94
  126.1 16.5 %copy.78 = f32[2,256,256]{0,2,1:T(8,128)} copy(f32[2,256,256]{2,1,0:T(8,128)S(1)} %get-tuple-element.573) | data formatting | bytes 1048576 | tf_op jit(solution)/shard_map/squeeze | solution.py:34
  142.5 2.3 gather_fusion.4
  145.0 16.4 %copy.80 = f32[2,256,256]{0,2,1:T(8,128)} copy(f32[2,256,256]{2,1,0:T(8,128)S(1)} %get-tuple-element.574) | data formatting | bytes 1048576 | tf_op jit(solution)/shard_map/squeeze | solution.py:35
  161.4 2.3 gather_fusion.5
  169.8 6.6 %all-to-all-start = ((f32[1,2,2,8,32,256]{5,1,4,2,0,3:T(2,128)}), f32[1,2,2,8,32,256]{5,1,4,2,0,3:T(2,128)S(1)}, u32[]{:S(2)}, u32[]{:S(2)}) async-start(f32[1,2,2,8,32,256]{5,1,4,2,0,3:T(2,128)} %pad_maximum_fusion.4), calls=%async_computation | async-start | bytes 2097152 | tf_op jit(solution)/shard_map/all_to_all | solution.py:229
  182.6 10.2 %all-to-all-done = f32[1,2,2,8,32,256]{5,1,4,2,0,3:T(2,128)S(1)} async-done(((f32[1,2,2,8,32,256]{5,1,4,2,0,3:T(2,128)}), f32[1,2,2,8,32,256]{5,1,4,2,0,3:T(2,128)S(1)}, u32[]{:S(2)}, u32[]{:S(2)}) %all-to-all-start) | async-done | bytes 1048608 | tf_op jit(solution)/shard_map/all_to_all | solution.py:229
  192.8 3.7 %multiply_add_fusion.6 = f32[8,2,2,32,256]{4,1,3,2,0:T(2,128)S(1)} fusion(s32[]{:T(128)S(6)} %select_n.58, f32[8,2,2,32,256]{4,1,3,2,0:T(2,128)S(1)} %bitcast.181, s32[]{:T(128)S(6)} %select_n.57, s32[]{:T(128)S(6)} %select_n.56, s32[]{:T(128)S(6)} %select_n.55, f32[]{:T(128)} %bitcast.46, f32[]{:T(128)} %bitcast.22), kind=kLoop, calls=%fused_computation.106 | loop fusion | flops 1310720 | bytes 2097176 | tf_op jit(solution)/shard_map/add | solution.py:126
  197.9 31.6 %all-gather.2.cloned.1.call-done = f32[8,4,2,32,256]{4,3,2,0,1:T(8,128)} async-done(((f32[8,2,2,32,256]{4,3,2,0,1:T(8,128)}), f32[8,4,2,32,256]{4,3,2,0,1:T(8,128)}) %all-gather.2.cloned.1.call-update) | async-done | bytes 2097168 | tf_op jit(solution)/shard_map/all_gather | solution.py:238
  229.5 6.5 %fusion.45 = f32[8,2,2,1,32,256]{5,1,4,2,3,0:T(2,128)S(1)} fusion(f32[8,4,2,32,256]{4,3,2,0,1:T(8,128)} %all-gather.2.cloned.1.call-done, f32[32,256]{1,0:T(8,128)S(1)} %convert_bitcast_fusion, f32[4,4]{1,0:T(4,128)S(1)} %bitcast.186, s32[]{:T(128)S(6)} %select_n.59), kind=kOutput, calls=%fused_computation.92 | convolution fusion | flops 12845056 | bytes 3179524 | tf_op jit(solution)/shard_map/kj,ej...->ek.../dot_general | solution.py:235
  236.1 30.9 %all_to_all.30 = f32[8,2,2,1,32,256]{5,1,4,2,3,0:T(2,128)S(1)} all-to-all(f32[8,2,2,1,32,256]{5,1,4,2,3,0:T(2,128)S(1)} %fusion.45), channel_id=1, replica_groups=mesh['space'=2,'energy'=8,'mom'=2] {'energy'}, dimensions={0} | all-to-all | bytes 2097152 | tf_op jit(solution)/shard_map/all_to_all | solution.py:243
  (145 shorter events, 57.8 us)
Async XLA Ops:
  6.5 191.1 %copy-start = (f32[4]{0:T(128)S(1)}, f32[4]{0:T(128)}, u32[]{:S(2)}) copy-start(f32[4]{0:T(128)} %param.29) | copy-start | bytes 52
  6.5 3.2 %copy-start.9 = (f32[1,256,256]{2,1,0:T(8,128)S(1)}, f32[1,256,256]{2,1,0:T(8,128)}, u32[]{:S(2)}) copy-start(f32[1,256,256]{2,1,0:T(8,128)} %param.24) | copy-start | bytes 786436
  6.6 3.4 %copy-start.7 = (f32[256,256]{1,0:T(8,128)}, f32[256,256]{1,0:T(8,128)S(1)}, u32[]{:S(2)}) copy-start(f32[256,256]{1,0:T(8,128)S(1)} %fusion.57) | copy-start | bytes 786436
  10.0 0.8 copy-start.4
  10.0 1.0 copy-start.5
  11.0 4.1 %copy-start.1 = (f32[1,224,224]{2,1,0:T(8,128)S(1)}, f32[1,224,224]{2,1,0:T(8,128)}, u32[]{:S(2)}) copy-start(f32[1,224,224]{2,1,0:T(8,128)} %param.25) | copy-start | bytes 602116
  11.1 1.0 copy-start.2
  15.1 3.8 %collective-permute-start = (f32[2,224,224]{2,1,0:T(8,128)S(1)}, f32[2,224,224]{2,1,0:T(8,128)S(1)}, u32[]{:S(2)}, u32[]{:S(2)}) collective-permute-start(f32[2,224,224]{2,1,0:T(8,128)S(1)} %get-tuple-element.708), channel_id=1, source_target_pairs={{0,16},{1,17},{2,18},{3,19},{4,20},{5,21},{6,22},{7,23},{8,24},{9,... | collective-permute-start | bytes 1204232 | tf_op jit(solution)/shard_map/while/body/eval_jaxpr/ppermute | solution.py:14
  30.2 2.7 collective-permute-start
  44.2 3.7 %collective-permute-start = (f32[2,224,224]{2,1,0:T(8,128)S(1)}, f32[2,224,224]{2,1,0:T(8,128)S(1)}, u32[]{:S(2)}, u32[]{:S(2)}) collective-permute-start(f32[2,224,224]{2,1,0:T(8,128)S(1)} %get-tuple-element.708), channel_id=1, source_target_pairs={{0,16},{1,17},{2,18},{3,19},{4,20},{5,21},{6,22},{7,23},{8,24},{9,... | collective-permute-start | bytes 1204232 | tf_op jit(solution)/shard_map/while/body/eval_jaxpr/ppermute | solution.py:14
  55.7 61.7 %copy-start.3 = (f32[2,2,256,256]{3,2,0,1:T(8,128)S(1)}, f32[2,2,256,256]{3,2,0,1:T(8,128)}, u32[]{:S(2)}) copy-start(f32[2,2,256,256]{3,2,0,1:T(8,128)} %scatter-add.16) | copy-start | bytes 3145732
  55.9 14.5 %collective-permute-start.1 = (f32[2,224,224]{1,2,0:T(8,128)S(1)}, f32[2,224,224]{1,2,0:T(8,128)}, u32[]{:S(2)}, u32[]{:S(2)}) collective-permute-start(f32[2,224,224]{1,2,0:T(8,128)S(1)} %copy.110), channel_id=1, source_target_pairs={{16,0},{17,1},{18,2},{19,3},{20,4},{21,5},{22,6},{23,7},{24,8},{25... | collective-permute-start | bytes 1204232 | tf_op jit(solution)/shard_map/while/body/eval_jaxpr/ppermute | solution.py:14
  70.6 16.1 %collective-permute-start.1 = (f32[2,224,224]{1,2,0:T(8,128)S(1)}, f32[2,224,224]{1,2,0:T(8,128)}, u32[]{:S(2)}, u32[]{:S(2)}) collective-permute-start(f32[2,224,224]{1,2,0:T(8,128)S(1)} %copy.110), channel_id=1, source_target_pairs={{16,0},{17,1},{18,2},{19,3},{20,4},{21,5},{22,6},{23,7},{24,8},{25... | collective-permute-start | bytes 1204232 | tf_op jit(solution)/shard_map/while/body/eval_jaxpr/ppermute | solution.py:14
  100.3 3.8 %collective-permute-start.1 = (f32[2,224,224]{1,2,0:T(8,128)S(1)}, f32[2,224,224]{1,2,0:T(8,128)}, u32[]{:S(2)}, u32[]{:S(2)}) collective-permute-start(f32[2,224,224]{1,2,0:T(8,128)S(1)} %copy.110), channel_id=1, source_target_pairs={{16,0},{17,1},{18,2},{19,3},{20,4},{21,5},{22,6},{23,7},{24,8},{25... | collective-permute-start | bytes 1204232 | tf_op jit(solution)/shard_map/while/body/eval_jaxpr/ppermute | solution.py:14
  144.9 18.9 %copy-start.6 = (f32[256,256]{1,0:T(8,128)S(1)}, f32[256,256]{1,0:T(8,128)}, u32[]{:S(2)}) copy-start(f32[256,256]{1,0:T(8,128)} %broadcast_subtract_fusion) | copy-start | bytes 786436
  166.3 1.0 copy-start.8
  167.4 9.3 %copy-start.11 = (s32[2]{0:T(128)S(1)}, s32[2]{0:T(128)}, u32[]{:S(2)}) copy-start(s32[2]{0:T(128)} %param.31) | copy-start | bytes 28
  167.4 14.6 %copy-start.12 = (f32[2]{0:T(128)S(1)}, f32[2]{0:T(128)}, u32[]{:S(2)}) copy-start(f32[2]{0:T(128)} %param.30) | copy-start | bytes 28
  169.8 23.0 %all-to-all-start = ((f32[1,2,2,8,32,256]{5,1,4,2,0,3:T(2,128)}), f32[1,2,2,8,32,256]{5,1,4,2,0,3:T(2,128)S(1)}, u32[]{:S(2)}, u32[]{:S(2)}) async-start(f32[1,2,2,8,32,256]{5,1,4,2,0,3:T(2,128)} %pad_maximum_fusion.4), calls=%async_computation | async-start | bytes 2097152 | tf_op jit(solution)/shard_map/all_to_all | solution.py:229
  176.4 21.3 %copy-start.13 = (s32[4,4]{1,0:T(4,128)S(1)}, s32[4,4]{1,0:T(4,128)}, u32[]{:S(2)}) copy-start(s32[4,4]{1,0:T(4,128)} %param.28) | copy-start | bytes 196
  176.4 21.5 %copy-start.10 = (s32[1,32,256]{2,1,0:T(8,128)S(1)}, s32[1,32,256]{2,1,0:T(8,128)}, u32[]{:S(2)}) copy-start(s32[1,32,256]{2,1,0:T(8,128)} %param.27) | copy-start | bytes 98308
  176.4 53.1 %all-gather.2.cloned.1.call-start = ((), (), s32[]{:S(2)}) async-start(), calls=%async_computation.2 | async-start | bytes 3145728 | tf_op jit(solution)/shard_map/all_gather | solution.py:238
Sparse Core Ops, SparseCore 0:
  197.8 31.6 all-gather.1
where the time goes:
time: 276 us; the launch traced here: 275 us
  local copies, waits for them, and re-layouts  93.8 us (34%)
  waiting for transfers between devices  76.4 us (28%)
  blocking collectives  30.9 us (11%)
  matrix products  24 us (9%)
  between operations  18.5 us (7%)
  starting transfers between devices  16.9 us (6%)
  other arithmetic  13.6 us (5%)
    ppermute x6, waiting for transfers between devices, from_behind(): return lax.ppermute(shard, axis, pairs)  34.6 us
    all_gather x1, waiting for transfers between devices, body(): lax.all_gather(phonon, 'mom', axis=1, tiled=True)  31.6 us
    all_to_all x1, blocking collectives, body(): lax.all_to_all(mixed_terms, 'energy', split_axis=0, concat_axis=3, tiled=...  30.9 us
    squeeze x6, local copies, waits for them, and re-layouts, approximate_inverse(): real_part = matrix[..., 0, :, :]  16.7 us
    squeeze x1, local copies, waits for them, and re-layouts, approximate_inverse(): imag_part = matrix[..., 1, :, :]  16.4 us
    scatter-add x3, local copies, waits for them, and re-layouts, embed_last(): return matrix.at[..., order_size - width:, order_size - width:].add(-term)  13.8 us
    gather x6, local copies, waits for them, and re-layouts, approximate_inverse(): diag_real = jnp.diagonal(real_part, axis1=-2, axis2=-1)  11.8 us
    gather x6, local copies, waits for them, and re-layouts, approximate_inverse(): diag_imag = jnp.diagonal(imag_part, axis1=-2, axis2=-1)  11.8 us
  transfers between devices with their start and end apart: 8, of which 8 were waited for; matrix products, arithmetic and copies ran while one was open for 0% of the time, Pallas kernels for 0%

commit v1 on v0

--- a/solution.py
+++ b/solution.py
@@ -6,6 +6,18 @@
 broadening = 1.0
 contact = 1.0
 dispersion = 1.0
+
+
+def doubled_up(array, axis, dim):
+    ways, here, step = (lax.axis_size(axis), lax.axis_index(axis), array.shape[dim])
+    line, have = (array, 1)
+    while have < ways:
+        line = jnp.concatenate(
+            [line, lax.ppermute(line, axis, [(d, (d - have) % ways) for d in range(ways)])],
+            axis=dim,
+        )
+        have = 2 * have
+    return jnp.roll(line, here * step, axis=dim)
 
 
 def from_behind(shard, axis, by):
@@ -233,10 +245,7 @@
         coefficients, lax.axis_index("mom") * momenta_here, momenta_here, 0
     )
     mixed_terms = jnp.zeros_like(phonon) + jnp.einsum(
-        "kj,ej...->ek...",
-        own_rows,
-        lax.all_gather(phonon, "mom", axis=1, tiled=True),
-        precision=lax.Precision.HIGHEST,
+        "kj,ej...->ek...", own_rows, doubled_up(phonon, "mom", 1), precision=lax.Precision.HIGHEST
     )
     mixed_terms = mixed_terms * mask_rows
     mixed_terms = mixed_terms.reshape(energies_all, momenta_here, 2, 1, row_count, orbitals)

time: 276 us -> 234 us (0.85)
  waiting for transfers between devices: 76.4 us -> 57.9 us
  between operations: 18.5 us -> 5.39 us
  blocking collectives: 30.9 us -> 18.9 us
    all_gather x1 -> x0, waiting for transfers between devices: 31.6 us -> none  [body(): lax.all_gather(phonon, 'mom', axis=1, tiled=True)]
    ppermute x0 -> x1, waiting for transfers between devices: none -> 13.1 us  [doubled_up(): lax.ppermute(line, axis, [(d, (d - have) % ways) for d in range(ways)])]
    all_to_all x1, blocking collectives: 30.9 us -> 18.9 us  [body(): lax.all_to_all(mixed_terms, 'energy', split_axis=0, concat_axis=3, tiled=...]
  transfers between devices with their start and end apart: 8 -> 8, of which waited for: 8 -> 8; matrix products, arithmetic and copies ran while one was open for 0% -> 1% of each run, Pallas kernels for 0% -> 0%
where the time goes in v1:
time: 234 us; the launch traced here: 233 us
  local copies, waits for them, and re-layouts  92.3 us (39%)
  waiting for transfers between devices  57.9 us (25%)
  matrix products  25.7 us (11%)
  blocking collectives  18.9 us (8%)
  starting transfers between devices  18.2 us (8%)
  other arithmetic  13.6 us (6%)
  between operations  5.39 us (2%)
    ppermute x6, waiting for transfers between devices, from_behind(): return lax.ppermute(shard, axis, pairs)  34.6 us
    all_to_all x1, blocking collectives, body(): lax.all_to_all(mixed_terms, 'energy', split_axis=0, concat_axis=3, tiled=...  18.9 us
    squeeze x6, local copies, waits for them, and re-layouts, approximate_inverse(): real_part = matrix[..., 0, :, :]  16.8 us
    squeeze x1, local copies, waits for them, and re-layouts, approximate_inverse(): imag_part = matrix[..., 1, :, :]  16.5 us
    scatter-add x3, local copies, waits for them, and re-layouts, embed_last(): return matrix.at[..., order_size - width:, order_size - width:].add(-term)  13.9 us
    ppermute x1, waiting for transfers between devices, doubled_up(): lax.ppermute(line, axis, [(d, (d - have) % ways) for d in range(ways)])  13.1 us
    gather x6, local copies, waits for them, and re-layouts, approximate_inverse(): diag_real = jnp.diagonal(real_part, axis1=-2, axis2=-1)  11.8 us
    gather x6, local copies, waits for them, and re-layouts, approximate_inverse(): diag_imag = jnp.diagonal(imag_part, axis1=-2, axis2=-1)  11.8 us
  transfers between devices with their start and end apart: 8, of which 8 were waited for; matrix products, arithmetic and copies ran while one was open for 1% of the time, Pallas kernels for 0%

profile of v1, /device:TPU:0, one launch (start us, length us, event | category | flops | bytes accessed | tf_op | source)
XLA Modules:
  0.0 232.8 jit_solution(16670871489499859884)
XLA Ops:
  7.9 32.8 %while.36 = (s32[]{:T(128)}, f32[2,2,224,224]{3,2,1,0:T(8,128)}, f32[2,224,224]{2,1,0:T(8,128)S(1)}, s32[]{:T(128)}, pred[]{:T(512)}, /*index=5*/f32[2,224,224]{...) while((s32[]{:T(128)}, f32[2,2,224,224]{3,2,1,0:T(8,128)}, ...), condition=%wide.region_3.0_spmd, body=%wide.region_0.3_spmd.sunk | while | flops 1347138048 | bytes 16336718 | solution.py:232
  7.9 2.4 %collective-permute-start = (f32[2,224,224]{2,1,0:T(8,128)S(1)}, f32[2,224,224]{2,1,0:T(8,128)S(1)}, u32[]{:S(2)}, u32[]{:S(2)}) collective-permute-start(f32[2,224,224]{2,1,0:T(8,128)S(1)} %get-tuple-element.708), channel_id=1, source_target_pairs={{0,16},{1,17},{2,18},{3,19},{4,20},{5,21},{6,22},{7,23},{8,24},{9,... | collective-permute-start | bytes 1204232 | tf_op jit(solution)/shard_map/while/body/eval_jaxpr/ppermute | solution.py:26
  11.7 11.3 %conditional.4 = ((f32[2,2,224,224]{3,2,1,0:T(8,128)}, f32[2,224,224]{2,1,0:T(8,128)S(1)})) conditional(s32[]{:T(128)} %convert_element_type.173, (f32[2,2,224,224]{3,2,1,0:T(8,128)}, f32[2,224,224]{2,1,0:T(8,128)S(1)}) %tuple.116, (pred[]{:T(512)}, f32[2,224,224]{2,1,0:T(8,128)S(1)}, f32[2,224,224]{2,1,0:T(8,128)S(1)}, s32[]{:T(128)}, ...), branch_computations={%region_1.0_spmd, %region_2.2_spmd} | conditional | flops 1347138048 | bytes 14730827 | solution.py:203
  14.2 2.3 %gather_fusion = f32[256]{0:T(256)S(1)} fusion(f32[256,256]{1,0:T(8,128)S(1)} %get-tuple-element.551, s32[256]{0:T(256)S(1)} %bitcast.174), kind=kCustom, calls=%fused_computation | custom fusion | bytes 4096 | tf_op jit(solution)/shard_map/while/body/eval_jaxpr/cond/branch_1_fun/jit(diagonal)/cond/branch_0_fun/gather | solution.py:48
  16.6 2.3 %gather_fusion.1 = f32[256]{0:T(256)S(1)} fusion(f32[256,256]{1,0:T(8,128)S(1)} %get-tuple-element.552, s32[256]{0:T(256)S(1)} %bitcast.175), kind=kCustom, calls=%fused_computation.1 | custom fusion | bytes 4096 | tf_op jit(solution)/shard_map/while/body/eval_jaxpr/cond/branch_1_fun/jit(diagonal)/cond/branch_0_fun/gather | solution.py:49
  25.7 11.3 %conditional.4 = ((f32[2,2,224,224]{3,2,1,0:T(8,128)}, f32[2,224,224]{2,1,0:T(8,128)S(1)})) conditional(s32[]{:T(128)} %convert_element_type.173, (f32[2,2,224,224]{3,2,1,0:T(8,128)}, f32[2,224,224]{2,1,0:T(8,128)S(1)}) %tuple.116, (pred[]{:T(512)}, f32[2,224,224]{2,1,0:T(8,128)S(1)}, f32[2,224,224]{2,1,0:T(8,128)S(1)}, s32[]{:T(128)}, ...), branch_computations={%region_1.0_spmd, %region_2.2_spmd} | conditional | flops 1347138048 | bytes 14730827 | solution.py:203
  28.2 2.3 %gather_fusion = f32[256]{0:T(256)S(1)} fusion(f32[256,256]{1,0:T(8,128)S(1)} %get-tuple-element.551, s32[256]{0:T(256)S(1)} %bitcast.174), kind=kCustom, calls=%fused_computation | custom fusion | bytes 4096 | tf_op jit(solution)/shard_map/while/body/eval_jaxpr/cond/branch_1_fun/jit(diagonal)/cond/branch_0_fun/gather | solution.py:48
  30.5 2.3 %gather_fusion.1 = f32[256]{0:T(256)S(1)} fusion(f32[256,256]{1,0:T(8,128)S(1)} %get-tuple-element.552, s32[256]{0:T(256)S(1)} %bitcast.175), kind=kCustom, calls=%fused_computation.1 | custom fusion | bytes 4096 | tf_op jit(solution)/shard_map/while/body/eval_jaxpr/cond/branch_1_fun/jit(diagonal)/cond/branch_0_fun/gather | solution.py:49
  42.2 5.2 %scatter-add.16 = f32[2,2,256,256]{3,2,0,1:T(8,128)} dynamic-update-slice(f32[2,2,256,256]{3,2,0,1:T(8,128)} %copy-done.2, f32[2,2,224,224]{3,2,0,1:T(8,128)S(1)} %fusion.58, s32[]{:T(128)} %constant.284.clone.1, s32[]{:T(128)} %constant.284.clone.1, s32[]{:T(128)} %constant.284.clone.1, s32[]{:T(128)} %constant.284.clone.1) | dynamic-update-slice | bytes 1605636 | tf_op jit(solution)/shard_map/scatter-add | solution.py:100
  48.5 61.7 %while.37 = (s32[]{:T(128)}, f32[2,2,224,224]{3,2,1,0:T(8,128)}, f32[2,224,224]{2,1,0:T(8,128)S(1)}, s32[]{:T(128)}, pred[]{:T(512)}, /*index=5*/f32[2,224,224]{...) while((s32[]{:T(128)}, f32[2,2,224,224]{3,2,1,0:T(8,128)}, ...), condition=%wide.region_7.8_spmd, body=%wide.region_4.7_spmd.sunk | while | flops 1347037696 | bytes 17139036 | solution.py:233
  50.2 13.1 %collective-permute-done.1 = f32[2,224,224]{1,2,0:T(8,128)} collective-permute-done((f32[2,224,224]{1,2,0:T(8,128)S(1)}, f32[2,224,224]{1,2,0:T(8,128)}, u32[]{:S(2)}, u32[]{:S(2)}) %collective-permute-start.1) | collective-permute-done | bytes 401440 | tf_op jit(solution)/shard_map/while/body/eval_jaxpr/ppermute | solution.py:26
  64.7 14.9 %collective-permute-done.1 = f32[2,224,224]{1,2,0:T(8,128)} collective-permute-done((f32[2,224,224]{1,2,0:T(8,128)S(1)}, f32[2,224,224]{1,2,0:T(8,128)}, u32[]{:S(2)}, u32[]{:S(2)}) %collective-permute-start.1) | collective-permute-done | bytes 401440 | tf_op jit(solution)/shard_map/while/body/eval_jaxpr/ppermute | solution.py:26
  79.6 13.3 %conditional.5 = ((f32[2,2,224,224]{3,2,1,0:T(8,128)}, f32[2,224,224]{2,1,0:T(8,128)S(1)})) conditional(s32[]{:T(128)} %convert_element_type.174, (f32[2,2,224,224]{3,2,1,0:T(8,128)}, f32[2,224,224]{2,1,0:T(8,128)S(1)}) %tuple.119, (pred[]{:T(512)}, f32[2,224,224]{1,2,0:T(8,128)}, f32[2,224,224]{1,2,0:T(8,128)}, f32[224,224]{1,0:T(8,128)S(1)}, ...), branch_computations={%region_5.5_spmd, %region_6.6_spmd} | conditional | flops 1347037696 | bytes 14730331 | solution.py:223
  82.8 3.4 %scatter-add.10 = f32[2,256,256]{2,1,0:T(8,128)S(1)} dynamic-update-slice(f32[2,256,256]{2,1,0:T(8,128)S(1)} %dynamic-slice_bitcast_fusion.2, f32[2,224,224]{2,1,0:T(8,128)S(1)} %fusion.22, s32[]{:T(128)} %constant.269.clone, s32[]{:T(128)} %constant.271.clone, s32[]{:T(128)} %constant.271.clone) | dynamic-update-slice | bytes 802820 | tf_op jit(solution)/shard_map/while/body/eval_jaxpr/cond/branch_1_fun/scatter-add | solution.py:106
  86.3 2.3 %gather_fusion.2 = f32[256]{0:T(256)S(1)} fusion(f32[256,256]{1,0:T(8,128)S(1)} %get-tuple-element.559, s32[256]{0:T(256)S(1)} %bitcast.176), kind=kCustom, calls=%fused_computation.2 | custom fusion | bytes 4096 | tf_op jit(solution)/shard_map/while/body/eval_jaxpr/cond/branch_1_fun/jit(diagonal)/cond/branch_0_fun/gather | solution.py:48
  88.6 2.3 %gather_fusion.3 = f32[256]{0:T(256)S(1)} fusion(f32[256,256]{1,0:T(8,128)S(1)} %get-tuple-element.560, s32[256]{0:T(256)S(1)} %bitcast.177), kind=kCustom, calls=%fused_computation.3 | custom fusion | bytes 4096 | tf_op jit(solution)/shard_map/while/body/eval_jaxpr/cond/branch_1_fun/jit(diagonal)/cond/branch_0_fun/gather | solution.py:49
  94.4 2.5 %collective-permute-done.1 = f32[2,224,224]{1,2,0:T(8,128)} collective-permute-done((f32[2,224,224]{1,2,0:T(8,128)S(1)}, f32[2,224,224]{1,2,0:T(8,128)}, u32[]{:S(2)}, u32[]{:S(2)}) %collective-permute-start.1) | collective-permute-done | bytes 401440 | tf_op jit(solution)/shard_map/while/body/eval_jaxpr/ppermute | solution.py:26
  96.9 13.3 %conditional.5 = ((f32[2,2,224,224]{3,2,1,0:T(8,128)}, f32[2,224,224]{2,1,0:T(8,128)S(1)})) conditional(s32[]{:T(128)} %convert_element_type.174, (f32[2,2,224,224]{3,2,1,0:T(8,128)}, f32[2,224,224]{2,1,0:T(8,128)S(1)}) %tuple.119, (pred[]{:T(512)}, f32[2,224,224]{1,2,0:T(8,128)}, f32[2,224,224]{1,2,0:T(8,128)}, f32[224,224]{1,0:T(8,128)S(1)}, ...), branch_computations={%region_5.5_spmd, %region_6.6_spmd} | conditional | flops 1347037696 | bytes 14730331 | solution.py:223
  100.2 3.4 %scatter-add.10 = f32[2,256,256]{2,1,0:T(8,128)S(1)} dynamic-update-slice(f32[2,256,256]{2,1,0:T(8,128)S(1)} %dynamic-slice_bitcast_fusion.2, f32[2,224,224]{2,1,0:T(8,128)S(1)} %fusion.22, s32[]{:T(128)} %constant.269.clone, s32[]{:T(128)} %constant.271.clone, s32[]{:T(128)} %constant.271.clone) | dynamic-update-slice | bytes 802820 | tf_op jit(solution)/shard_map/while/body/eval_jaxpr/cond/branch_1_fun/scatter-add | solution.py:106
  103.6 2.3 %gather_fusion.2 = f32[256]{0:T(256)S(1)} fusion(f32[256,256]{1,0:T(8,128)S(1)} %get-tuple-element.559, s32[256]{0:T(256)S(1)} %bitcast.176), kind=kCustom, calls=%fused_computation.2 | custom fusion | bytes 4096 | tf_op jit(solution)/shard_map/while/body/eval_jaxpr/cond/branch_1_fun/jit(diagonal)/cond/branch_0_fun/gather | solution.py:48
  106.0 2.3 %gather_fusion.3 = f32[256]{0:T(256)S(1)} fusion(f32[256,256]{1,0:T(8,128)S(1)} %get-tuple-element.560, s32[256]{0:T(256)S(1)} %bitcast.177), kind=kCustom, calls=%fused_computation.3 | custom fusion | bytes 4096 | tf_op jit(solution)/shard_map/while/body/eval_jaxpr/cond/branch_1_fun/jit(diagonal)/cond/branch_0_fun/gather | solution.py:49
  111.8 7.1 %scatter-add.17 = f32[2,2,256,256]{3,2,0,1:T(8,128)S(1)} dynamic-update-slice(f32[2,2,256,256]{3,2,0,1:T(8,128)S(1)} %copy-done.3, f32[2,2,224,224]{3,2,0,1:T(8,128)S(1)} %slice_add_fusion, s32[]{:T(128)} %constant.284.clone.1, s32[]{:T(128)} %constant.284.clone.1, s32[]{:T(128)} %constant.289.clone.1, s32[]{:T(128)} %constant.289.clone.1) | dynamic-update-slice | bytes 1605636 | tf_op jit(solution)/shard_map/scatter-add | solution.py:106
  118.9 16.5 %copy.76 = f32[2,256,256]{0,2,1:T(8,128)} copy(f32[2,256,256]{2,1,0:T(8,128)S(1)} %get-tuple-element.573) | data formatting | bytes 1048576 | tf_op jit(solution)/shard_map/squeeze | solution.py:46
  135.5 2.3 %gather_fusion.4 = f32[256,2]{1,0:T(8,128)S(1)} fusion(f32[2,256,256]{0,2,1:T(8,128)} %copy.76, s32[256]{0:T(256)S(1)} %bitcast.179), kind=kCustom, calls=%fused_computation.4 | custom fusion | bytes 6144 | tf_op jit(solution)/shard_map/jit(diagonal)/gather | solution.py:48
  137.9 16.5 %copy.78 = f32[2,256,256]{0,2,1:T(8,128)} copy(f32[2,256,256]{2,1,0:T(8,128)S(1)} %get-tuple-element.574) | data formatting | bytes 1048576 | tf_op jit(solution)/shard_map/squeeze | solution.py:47
  154.4 2.3 %gather_fusion.5 = f32[256,2]{1,0:T(8,128)S(1)} fusion(f32[2,256,256]{0,2,1:T(8,128)} %copy.78, s32[256]{0:T(256)S(1)} %bitcast.180), kind=kCustom, calls=%fused_computation.5 | custom fusion | bytes 6144 | tf_op jit(solution)/shard_map/jit(diagonal)/gather | solution.py:49
  162.8 6.7 %all-to-all-start = ((f32[1,2,2,8,32,256]{5,1,4,2,0,3:T(2,128)}), f32[1,2,2,8,32,256]{5,1,4,2,0,3:T(2,128)S(1)}, u32[]{:S(2)}, u32[]{:S(2)}) async-start(f32[1,2,2,8,32,256]{5,1,4,2,0,3:T(2,128)} %pad_maximum_fusion.4), calls=%async_computation | async-start | bytes 2097152 | tf_op jit(solution)/shard_map/all_to_all | solution.py:241
  175.7 10.2 %all-to-all-done = f32[1,2,2,8,32,256]{5,1,4,2,0,3:T(2,128)S(1)} async-done(((f32[1,2,2,8,32,256]{5,1,4,2,0,3:T(2,128)}), f32[1,2,2,8,32,256]{5,1,4,2,0,3:T(2,128)S(1)}, u32[]{:S(2)}, u32[]{:S(2)}) %all-to-all-start) | async-done | bytes 1048608 | tf_op jit(solution)/shard_map/all_to_all | solution.py:241
  185.9 3.7 %multiply_add_fusion.6 = f32[8,2,2,32,256]{4,1,3,2,0:T(2,128)S(1)} fusion(s32[]{:T(128)S(6)} %select_n.71, f32[8,2,2,32,256]{4,1,3,2,0:T(2,128)S(1)} %bitcast.181, s32[]{:T(128)S(6)} %select_n.70, s32[]{:T(128)S(6)} %select_n.69, s32[]{:T(128)S(6)} %select_n.68, f32[]{:T(128)} %bitcast.46, f32[]{:T(128)} %bitcast.22), kind=kLoop, calls=%fused_computation.112 | loop fusion | flops 1310720 | bytes 2097176 | tf_op jit(solution)/shard_map/add | solution.py:138
  191.4 13.1 %collective-permute-done.2 = f32[8,2,2,32,256]{4,1,3,2,0:T(2,128)S(1)} collective-permute-done((f32[8,2,2,32,256]{4,1,3,2,0:T(2,128)S(1)}, f32[8,2,2,32,256]{4,1,3,2,0:T(2,128)S(1)}, u32[]{:S(2)}, u32[]{:S(2)}) %collective-permute-start.2) | collective-permute-done | bytes 1048608 | tf_op jit(solution)/shard_map/ppermute | solution.py:16
  204.5 8.2 %fusion.48 = f32[8,2,2,1,32,256]{5,1,4,2,3,0:T(2,128)S(1)} fusion(s32[]{:T(128)S(6)} %select_n.73, f32[8,2,2,32,256]{4,1,3,2,0:T(2,128)S(1)} %multiply_add_fusion.6, f32[8,2,2,32,256]{4,1,3,2,0:T(2,128)S(1)} %collective-permute-done.2, f32[32,256]{1,0:T(8,128)S(1)} %convert_bitcast_fusion, f32[4,4]{1,0:T(4,128)S(1)} %bitcast.186, s32[]{:T(128)S(6)} %select_n.74), kind=kOutput, calls=%fused_computation.101 | convolution fusion | flops 14417920 | bytes 3179528 | tf_op jit(solution)/shard_map/kj,ej...->ek.../dot_general | solution.py:247
  212.8 18.9 %all_to_all.30 = f32[8,2,2,1,32,256]{5,1,4,2,3,0:T(2,128)S(1)} all-to-all(f32[8,2,2,1,32,256]{5,1,4,2,3,0:T(2,128)S(1)} %fusion.48), channel_id=1, replica_groups=mesh['space'=2,'energy'=8,'mom'=2] {'energy'}, dimensions={0} | all-to-all | bytes 2097152 | tf_op jit(solution)/shard_map/all_to_all | solution.py:252
  (143 shorter events, 57.4 us)
Async XLA Ops:
  0.0 191.2 %copy-start = (f32[4]{0:T(128)S(1)}, f32[4]{0:T(128)}, u32[]{:S(2)}) copy-start(f32[4]{0:T(128)} %param.29) | copy-start | bytes 52
  0.0 3.2 %copy-start.9 = (f32[1,256,256]{2,1,0:T(8,128)S(1)}, f32[1,256,256]{2,1,0:T(8,128)}, u32[]{:S(2)}) copy-start(f32[1,256,256]{2,1,0:T(8,128)} %param.24) | copy-start | bytes 786436
  0.0 3.4 %copy-start.7 = (f32[256,256]{1,0:T(8,128)}, f32[256,256]{1,0:T(8,128)S(1)}, u32[]{:S(2)}) copy-start(f32[256,256]{1,0:T(8,128)S(1)} %fusion.60) | copy-start | bytes 786436
  3.5 0.8 copy-start.4
  3.5 1.0 copy-start.5
  3.5 4.4 %copy-start.1 = (f32[1,224,224]{2,1,0:T(8,128)S(1)}, f32[1,224,224]{2,1,0:T(8,128)}, u32[]{:S(2)}) copy-start(f32[1,224,224]{2,1,0:T(8,128)} %param.25) | copy-start | bytes 602116
  3.6 1.2 copy-start.2
  7.9 3.8 %collective-permute-start = (f32[2,224,224]{2,1,0:T(8,128)S(1)}, f32[2,224,224]{2,1,0:T(8,128)S(1)}, u32[]{:S(2)}, u32[]{:S(2)}) collective-permute-start(f32[2,224,224]{2,1,0:T(8,128)S(1)} %get-tuple-element.708), channel_id=1, source_target_pairs={{0,16},{1,17},{2,18},{3,19},{4,20},{5,21},{6,22},{7,23},{8,24},{9,... | collective-permute-start | bytes 1204232 | tf_op jit(solution)/shard_map/while/body/eval_jaxpr/ppermute | solution.py:26
  23.0 2.7 %collective-permute-start = (f32[2,224,224]{2,1,0:T(8,128)S(1)}, f32[2,224,224]{2,1,0:T(8,128)S(1)}, u32[]{:S(2)}, u32[]{:S(2)}) collective-permute-start(f32[2,224,224]{2,1,0:T(8,128)S(1)} %get-tuple-element.708), channel_id=1, source_target_pairs={{0,16},{1,17},{2,18},{3,19},{4,20},{5,21},{6,22},{7,23},{8,24},{9,... | collective-permute-start | bytes 1204232 | tf_op jit(solution)/shard_map/while/body/eval_jaxpr/ppermute | solution.py:26
  37.0 3.7 %collective-permute-start = (f32[2,224,224]{2,1,0:T(8,128)S(1)}, f32[2,224,224]{2,1,0:T(8,128)S(1)}, u32[]{:S(2)}, u32[]{:S(2)}) collective-permute-start(f32[2,224,224]{2,1,0:T(8,128)S(1)} %get-tuple-element.708), channel_id=1, source_target_pairs={{0,16},{1,17},{2,18},{3,19},{4,20},{5,21},{6,22},{7,23},{8,24},{9,... | collective-permute-start | bytes 1204232 | tf_op jit(solution)/shard_map/while/body/eval_jaxpr/ppermute | solution.py:26
  48.5 61.8 %copy-start.3 = (f32[2,2,256,256]{3,2,0,1:T(8,128)S(1)}, f32[2,2,256,256]{3,2,0,1:T(8,128)}, u32[]{:S(2)}) copy-start(f32[2,2,256,256]{3,2,0,1:T(8,128)} %scatter-add.16) | copy-start | bytes 3145732
  48.7 14.5 %collective-permute-start.1 = (f32[2,224,224]{1,2,0:T(8,128)S(1)}, f32[2,224,224]{1,2,0:T(8,128)}, u32[]{:S(2)}, u32[]{:S(2)}) collective-permute-start(f32[2,224,224]{1,2,0:T(8,128)S(1)} %copy.100), channel_id=1, source_target_pairs={{16,0},{17,1},{18,2},{19,3},{20,4},{21,5},{22,6},{23,7},{24,8},{25... | collective-permute-start | bytes 1204232 | tf_op jit(solution)/shard_map/while/body/eval_jaxpr/ppermute | solution.py:26
  63.4 16.2 %collective-permute-start.1 = (f32[2,224,224]{1,2,0:T(8,128)S(1)}, f32[2,224,224]{1,2,0:T(8,128)}, u32[]{:S(2)}, u32[]{:S(2)}) collective-permute-start(f32[2,224,224]{1,2,0:T(8,128)S(1)} %copy.100), channel_id=1, source_target_pairs={{16,0},{17,1},{18,2},{19,3},{20,4},{21,5},{22,6},{23,7},{24,8},{25... | collective-permute-start | bytes 1204232 | tf_op jit(solution)/shard_map/while/body/eval_jaxpr/ppermute | solution.py:26
  93.1 3.8 %collective-permute-start.1 = (f32[2,224,224]{1,2,0:T(8,128)S(1)}, f32[2,224,224]{1,2,0:T(8,128)}, u32[]{:S(2)}, u32[]{:S(2)}) collective-permute-start(f32[2,224,224]{1,2,0:T(8,128)S(1)} %copy.100), channel_id=1, source_target_pairs={{16,0},{17,1},{18,2},{19,3},{20,4},{21,5},{22,6},{23,7},{24,8},{25... | collective-permute-start | bytes 1204232 | tf_op jit(solution)/shard_map/while/body/eval_jaxpr/ppermute | solution.py:26
  137.9 19.0 %copy-start.6 = (f32[256,256]{1,0:T(8,128)S(1)}, f32[256,256]{1,0:T(8,128)}, u32[]{:S(2)}) copy-start(f32[256,256]{1,0:T(8,128)} %broadcast_subtract_fusion) | copy-start | bytes 786436
  159.4 1.0 copy-start.8
  160.5 9.0 %copy-start.11 = (s32[2]{0:T(128)S(1)}, s32[2]{0:T(128)}, u32[]{:S(2)}) copy-start(s32[2]{0:T(128)} %param.31) | copy-start | bytes 28
  160.5 14.6 %copy-start.12 = (f32[2]{0:T(128)S(1)}, f32[2]{0:T(128)}, u32[]{:S(2)}) copy-start(f32[2]{0:T(128)} %param.30) | copy-start | bytes 28
  161.3 29.9 %copy-start.13 = (s32[4,4]{1,0:T(4,128)S(1)}, s32[4,4]{1,0:T(4,128)}, u32[]{:S(2)}) copy-start(s32[4,4]{1,0:T(4,128)} %param.28) | copy-start | bytes 196
  161.3 30.1 %copy-start.10 = (s32[1,32,256]{2,1,0:T(8,128)S(1)}, s32[1,32,256]{2,1,0:T(8,128)}, u32[]{:S(2)}) copy-start(s32[1,32,256]{2,1,0:T(8,128)} %param.27) | copy-start | bytes 98308
  162.8 23.0 %all-to-all-start = ((f32[1,2,2,8,32,256]{5,1,4,2,0,3:T(2,128)}), f32[1,2,2,8,32,256]{5,1,4,2,0,3:T(2,128)S(1)}, u32[]{:S(2)}, u32[]{:S(2)}) async-start(f32[1,2,2,8,32,256]{5,1,4,2,0,3:T(2,128)} %pad_maximum_fusion.4), calls=%async_computation | async-start | bytes 2097152 | tf_op jit(solution)/shard_map/all_to_all | solution.py:241
  189.7 14.9 %collective-permute-start.2 = (f32[8,2,2,32,256]{4,1,3,2,0:T(2,128)S(1)}, f32[8,2,2,32,256]{4,1,3,2,0:T(2,128)S(1)}, u32[]{:S(2)}, u32[]{:S(2)}) collective-permute-start(f32[8,2,2,32,256]{4,1,3,2,0:T(2,128)S(1)} %multiply_add_fusion.6), channel_id=1, source_target_pairs={{0,1},{1,0},{2,3},{3,2},{4,5},{5,4},{6,7},{7,6},{8,9},{9,8},{10,11... | collective-permute-start | bytes 3145736 | tf_op jit(solution)/shard_map/ppermute | solution.py:16
